TPU v7x, 256 devices: a whole 4x4x8 slice. The times are simulated.
256 devices in a mesh: row: 8 (over z), col: 32 (over y, x, core).
Axes of the slice: x: 4, y: 4, z: 8, core: 2. Of those that a mesh axis runs over, the one named last changes fastest.
Arguments:
- factor: bfloat16 [32, 8, 8, 32, 128, 128], P(None, 'row', None, 'col'), may hold values from -0.046875 to 0.046875
- pattern: int32 [32, 8, 8, 32], P(None, 'row', None, 'col'), may hold values 0 or 1
- loads: float32 [8, 32, 128, 256], P(None, 'col'), may hold values from -6 to 6
- block_inverse: float32 [8, 32, 128, 128], P(None, 'col'), may hold values from -1 to 2, as said below
Outputs:
- solution: float32 [8, 32, 128, 256], P(None, 'col')
Inputs may be any that keep to these rules, and one draw needn't show every extreme that they name: `block_inverse`: each block is lower triangular with diagonal entries between 0.5 and 1.5.
All inputs are finite; a program needn't handle non-finite values. No bound on the sum of `pattern` on one device may be relied on, other than what follows from the above.
Results may differ from a plain program's by a relative error of at most 0.0045.
Values may be sent and summed in bfloat16 or wider, within the bound.
No kernel may reach another device: no remote copies, remote signals or barrier semaphores. Data moves between devices by JAX's collectives and lax.ppermute only.
A program may use at most 128 MiB of HBM per device.

v0:
```python
import jax
import jax.numpy as jnp
from jax import lax
from jax.sharding import PartitionSpec as P

LEVELS = 8


def spread(value, axis, source):
    kept = jnp.where(lax.axis_index(axis) == source, value, 0).astype(value.dtype)
    return lax.psum(kept, axis)


def per_device(factor, pattern, loads, block_inverse):
    row_count = lax.axis_size("row")
    col_count = lax.axis_size("col")
    groups = col_count // row_count
    my_row = lax.axis_index("row")
    my_col = lax.axis_index("col")
    masked = factor[:, 0, :, 0] * pattern[:, 0, :, 0].astype(jnp.bfloat16)[:, :, None, None]
    per_row = factor.shape[0] // LEVELS
    per_col = factor.shape[2] // LEVELS
    rhs_local = loads[:, 0]
    inverse_local = block_inverse[:, 0]
    forward_vals = []
    forward_low = []
    for level_id in range(LEVELS):
        rhs_level = rhs_local[level_id * per_col : (level_id + 1) * per_col]
        inverse_level = inverse_local[level_id * per_col : (level_id + 1) * per_col]
        if level_id > 0:
            panel = masked[level_id * per_row : (level_id + 1) * per_row, : level_id * per_col]
            earlier = jnp.concatenate(forward_low, axis=0)
            partial_sum = jnp.einsum(
                "abpq,bqs->aps", panel, earlier, preferred_element_type=jnp.float32
            )
            row_total = lax.psum(partial_sum, "col")
            row_total = row_total.reshape((per_col, groups) + row_total.shape[1:])
            own_total = lax.dynamic_index_in_dim(
                row_total, my_col // row_count, axis=1, keepdims=False
            )
            solved = jnp.einsum(
                "mpq,mqs->mps",
                inverse_level,
                rhs_level - own_total,
                precision=lax.Precision.HIGHEST,
            )
            solved = spread(solved, "row", my_col % row_count)
        else:
            solved = jnp.einsum(
                "mpq,mqs->mps", inverse_level, rhs_level, precision=lax.Precision.HIGHEST
            )
        forward_vals.append(solved)
        forward_low.append(solved.astype(jnp.bfloat16))
    solution_parts = [None] * LEVELS
    later = []
    for level_id in reversed(range(LEVELS)):
        inverse_level = inverse_local[level_id * per_col : (level_id + 1) * per_col]
        resid = forward_vals[level_id]
        if level_id < LEVELS - 1:
            panel = masked[
                (level_id + 1) * per_row :, level_id * per_col : (level_id + 1) * per_col
            ]
            after = jnp.concatenate(later, axis=0)
            partial_sum = jnp.einsum(
                "abpq,aps->bqs", panel, after, preferred_element_type=jnp.float32
            )
            resid = resid - lax.psum(partial_sum, "row")
        solved = jnp.einsum("mqp,mqs->mps", inverse_level, resid, precision=lax.Precision.HIGHEST)
        solution_parts[level_id] = solved
        if level_id > 0:
            low_solved = solved.astype(jnp.bfloat16)
            pieces = lax.all_gather(low_solved[None], "col", axis=0, tiled=True)
            pieces = pieces.reshape((groups, row_count) + low_solved.shape)
            picked = lax.dynamic_index_in_dim(pieces, my_row, axis=1, keepdims=False)
            arranged = jnp.swapaxes(picked, 0, 1).reshape((per_row,) + low_solved.shape[1:])
            later = [arranged] + later
    solution = jnp.concatenate(solution_parts, axis=0)
    return solution[:, None]


def solution(mesh):
    in_specs = (
        P(None, "row", None, "col", None, None),
        P(None, "row", None, "col"),
        P(None, "col", None, None),
        P(None, "col", None, None),
    )
    out_specs = P(None, "col", None, None)
    return jax.shard_map(
        per_device, mesh=mesh, in_specs=in_specs, out_specs=out_specs, check_vma=False
    )
```

profile of v0, /device:TPU:2, one launch (start us, length us, event | category | flops | bytes accessed | tf_op | source)
XLA Modules:
  0.0 2246.1 jit_solution(3896068341786399089)
XLA Ops:
  8.5 7.4 bitcast_multiply_fusion
  17.9 116.1 %all-reduce.22.cloned.1.call-done = f32[4,128,256]{2,1,0:T(8,128)} async-done(((f32[4,128,256]{2,1,0:T(8,128)}), f32[4,128,256]{2,1,0:T(8,128)}) %all-reduce.22.cloned.1.call-update) | async-done | bytes 524304 | tf_op jit(solution)/shard_map/psum | solution.py:36
  135.9 72.4 %all-reduce.24.cloned.1.call-done = f32[1,128,256]{2,1,0:T(8,128)} async-done(((f32[1,128,256]{2,1,0:T(8,128)}), f32[1,128,256]{2,1,0:T(8,128)}) %all-reduce.24.cloned.1.call-update) | async-done | bytes 131088 | tf_op jit(solution)/shard_map/psum | solution.py:11
  211.3 111.8 %all-reduce.26.cloned.1.call-done = f32[4,128,256]{2,1,0:T(8,128)} async-done(((f32[4,128,256]{2,1,0:T(8,128)}), f32[4,128,256]{2,1,0:T(8,128)}) %all-reduce.26.cloned.1.call-update) | async-done | bytes 524304 | tf_op jit(solution)/shard_map/psum | solution.py:36
  325.1 72.3 %all-reduce.28.cloned.1.call-done = f32[1,128,256]{2,1,0:T(8,128)} async-done(((f32[1,128,256]{2,1,0:T(8,128)}), f32[1,128,256]{2,1,0:T(8,128)}) %all-reduce.28.cloned.1.call-update) | async-done | bytes 131088 | tf_op jit(solution)/shard_map/psum | solution.py:11
  400.5 111.6 %all-reduce.30.cloned.1.call-done = f32[4,128,256]{2,1,0:T(8,128)} async-done(((f32[4,128,256]{2,1,0:T(8,128)}), f32[4,128,256]{2,1,0:T(8,128)}) %all-reduce.30.cloned.1.call-update) | async-done | bytes 524304 | tf_op jit(solution)/shard_map/psum | solution.py:36
  514.0 72.3 %all-reduce.32.cloned.1.call-done = f32[1,128,256]{2,1,0:T(8,128)} async-done(((f32[1,128,256]{2,1,0:T(8,128)}), f32[1,128,256]{2,1,0:T(8,128)}) %all-reduce.32.cloned.1.call-update) | async-done | bytes 131088 | tf_op jit(solution)/shard_map/psum | solution.py:11
  589.5 111.6 %all-reduce.34.cloned.1.call-done = f32[4,128,256]{2,1,0:T(8,128)} async-done(((f32[4,128,256]{2,1,0:T(8,128)}), f32[4,128,256]{2,1,0:T(8,128)}) %all-reduce.34.cloned.1.call-update) | async-done | bytes 524304 | tf_op jit(solution)/shard_map/psum | solution.py:36
  703.1 72.4 %all-reduce.36.cloned.1.call-done = f32[1,128,256]{2,1,0:T(8,128)} async-done(((f32[1,128,256]{2,1,0:T(8,128)}), f32[1,128,256]{2,1,0:T(8,128)}) %all-reduce.36.cloned.1.call-update) | async-done | bytes 131088 | tf_op jit(solution)/shard_map/psum | solution.py:11
  778.8 111.6 %all-reduce.38.cloned.1.call-done = f32[4,128,256]{2,1,0:T(8,128)} async-done(((f32[4,128,256]{2,1,0:T(8,128)}), f32[4,128,256]{2,1,0:T(8,128)}) %all-reduce.38.cloned.1.call-update) | async-done | bytes 524304 | tf_op jit(solution)/shard_map/psum | solution.py:36
  892.3 72.3 %all-reduce.40.cloned.1.call-done = f32[1,128,256]{2,1,0:T(8,128)} async-done(((f32[1,128,256]{2,1,0:T(8,128)}), f32[1,128,256]{2,1,0:T(8,128)}) %all-reduce.40.cloned.1.call-update) | async-done | bytes 131088 | tf_op jit(solution)/shard_map/psum | solution.py:11
  965.6 2.3 convolution_bitcast_fusion.1
  967.9 111.7 %all-reduce.42.cloned.1.call-done = f32[4,128,256]{2,1,0:T(8,128)} async-done(((f32[4,128,256]{2,1,0:T(8,128)}), f32[4,128,256]{2,1,0:T(8,128)}) %all-reduce.42.cloned.1.call-update) | async-done | bytes 524304 | tf_op jit(solution)/shard_map/psum | solution.py:36
  1081.5 72.3 %all-reduce.44.cloned.1.call-done = f32[1,128,256]{2,1,0:T(8,128)} async-done(((f32[1,128,256]{2,1,0:T(8,128)}), f32[1,128,256]{2,1,0:T(8,128)}) %all-reduce.44.cloned.1.call-update) | async-done | bytes 131088 | tf_op jit(solution)/shard_map/psum | solution.py:11
  1154.8 2.4 convolution_bitcast_fusion
  1157.2 111.7 %all-reduce.46.cloned.1.call-done = f32[4,128,256]{2,1,0:T(8,128)} async-done(((f32[4,128,256]{2,1,0:T(8,128)}), f32[4,128,256]{2,1,0:T(8,128)}) %all-reduce.46.cloned.1.call-update) | async-done | bytes 524304 | tf_op jit(solution)/shard_map/psum | solution.py:36
  1270.8 72.3 %all-reduce.48.cloned.1.call-done = f32[128,256]{1,0:T(8,128)} async-done(((f32[128,256]{1,0:T(8,128)}), f32[128,256]{1,0:T(8,128)}) %all-reduce.48.cloned.1.call-update) | async-done | bytes 131088 | tf_op jit(solution)/shard_map/psum | solution.py:11
  1345.2 48.3 %all-gather.15.cloned.1.call-done = bf16[4096,256]{0,1:T(8,128)(2,1)} async-done(((bf16[128,256]{0,1:T(8,128)(2,1)}), bf16[4096,256]{0,1:T(8,128)(2,1)}) %all-gather.15.cloned.1.call-update) | async-done | bytes 2097168 | tf_op jit(solution)/shard_map/all_gather | solution.py:72
  1398.4 71.8 %all-reduce.50.cloned.1.call-done = f32[1,128,256]{2,1,0:T(8,128)} async-done(((f32[1,128,256]{2,1,0:T(8,128)}), f32[1,128,256]{2,1,0:T(8,128)}) %all-reduce.50.cloned.1.call-update) | async-done | bytes 131088 | tf_op jit(solution)/shard_map/psum | solution.py:67
  1472.2 48.6 %all-gather.17.cloned.1.call-done = bf16[4096,256]{0,1:T(8,128)(2,1)} async-done(((bf16[128,256]{0,1:T(8,128)(2,1)}), bf16[4096,256]{0,1:T(8,128)(2,1)}) %all-gather.17.cloned.1.call-update) | async-done | bytes 2097168 | tf_op jit(solution)/shard_map/all_gather | solution.py:72
  1525.9 71.8 %all-reduce.52.cloned.1.call-done = f32[1,128,256]{2,1,0:T(8,128)} async-done(((f32[1,128,256]{2,1,0:T(8,128)}), f32[1,128,256]{2,1,0:T(8,128)}) %all-reduce.52.cloned.1.call-update) | async-done | bytes 131088 | tf_op jit(solution)/shard_map/psum | solution.py:67
  1599.6 48.4 %all-gather.19.cloned.1.call-done = bf16[4096,256]{0,1:T(8,128)(2,1)} async-done(((bf16[128,256]{0,1:T(8,128)(2,1)}), bf16[4096,256]{0,1:T(8,128)(2,1)}) %all-gather.19.cloned.1.call-update) | async-done | bytes 2097168 | tf_op jit(solution)/shard_map/all_gather | solution.py:72
  1653.2 71.8 %all-reduce.54.cloned.1.call-done = f32[1,128,256]{2,1,0:T(8,128)} async-done(((f32[1,128,256]{2,1,0:T(8,128)}), f32[1,128,256]{2,1,0:T(8,128)}) %all-reduce.54.cloned.1.call-update) | async-done | bytes 131088 | tf_op jit(solution)/shard_map/psum | solution.py:67
  1727.2 48.6 %all-gather.21.cloned.1.call-done = bf16[4096,256]{0,1:T(8,128)(2,1)} async-done(((bf16[128,256]{0,1:T(8,128)(2,1)}), bf16[4096,256]{0,1:T(8,128)(2,1)}) %all-gather.21.cloned.1.call-update) | async-done | bytes 2097168 | tf_op jit(solution)/shard_map/all_gather | solution.py:72
  1781.1 71.8 %all-reduce.56.cloned.1.call-done = f32[1,128,256]{2,1,0:T(8,128)} async-done(((f32[1,128,256]{2,1,0:T(8,128)}), f32[1,128,256]{2,1,0:T(8,128)}) %all-reduce.56.cloned.1.call-update) | async-done | bytes 131088 | tf_op jit(solution)/shard_map/psum | solution.py:67
  1854.9 48.4 %all-gather.23.cloned.1.call-done = bf16[4096,256]{0,1:T(8,128)(2,1)} async-done(((bf16[128,256]{0,1:T(8,128)(2,1)}), bf16[4096,256]{0,1:T(8,128)(2,1)}) %all-gather.23.cloned.1.call-update) | async-done | bytes 2097168 | tf_op jit(solution)/shard_map/all_gather | solution.py:72
  1908.8 71.8 %all-reduce.58.cloned.1.call-done = f32[1,128,256]{2,1,0:T(8,128)} async-done(((f32[1,128,256]{2,1,0:T(8,128)}), f32[1,128,256]{2,1,0:T(8,128)}) %all-reduce.58.cloned.1.call-update) | async-done | bytes 131088 | tf_op jit(solution)/shard_map/psum | solution.py:67
  1982.6 48.7 %all-gather.25.cloned.1.call-done = bf16[4096,256]{0,1:T(8,128)(2,1)} async-done(((bf16[128,256]{0,1:T(8,128)(2,1)}), bf16[4096,256]{0,1:T(8,128)(2,1)}) %all-gather.25.cloned.1.call-update) | async-done | bytes 2097168 | tf_op jit(solution)/shard_map/all_gather | solution.py:72
  2036.8 71.8 %all-reduce.60.cloned.1.call-done = f32[1,128,256]{2,1,0:T(8,128)} async-done(((f32[1,128,256]{2,1,0:T(8,128)}), f32[1,128,256]{2,1,0:T(8,128)}) %all-reduce.60.cloned.1.call-update) | async-done | bytes 131088 | tf_op jit(solution)/shard_map/psum | solution.py:67
  2110.7 48.2 %all-gather.27.cloned.1.call-done = bf16[4096,256]{0,1:T(8,128)(2,1)} async-done(((bf16[128,256]{0,1:T(8,128)(2,1)}), bf16[4096,256]{0,1:T(8,128)(2,1)}) %all-gather.27.cloned.1.call-update) | async-done | bytes 2097168 | tf_op jit(solution)/shard_map/all_gather | solution.py:72
  2162.2 2.4 convolution_bitcast_fusion.6
  2164.6 71.8 %all-reduce.62.cloned.1.call-done = f32[1,128,256]{2,1,0:T(8,128)} async-done(((f32[1,128,256]{2,1,0:T(8,128)}), f32[1,128,256]{2,1,0:T(8,128)}) %all-reduce.62.cloned.1.call-update) | async-done | bytes 131088 | tf_op jit(solution)/shard_map/psum | solution.py:67
  (165 shorter events, 82.8 us)
Async XLA Ops:
  6.5 127.4 %all-reduce.22.cloned.1.call-start = ((), (), s32[]{:S(2)}) async-start(), calls=%async_computation | async-start | bytes 1048576 | tf_op jit(solution)/shard_map/psum | solution.py:36
  8.4 125.5 %copy-start = (f32[8,1,128,128]{3,2,1,0:T(8,128)S(1)}, f32[8,1,128,128]{3,2,1,0:T(8,128)}, u32[]{:S(2)}) copy-start(f32[8,1,128,128]{3,2,1,0:T(8,128)} %param.7) | copy-start | bytes 1572868
  8.5 125.5 %copy-start.1 = (f32[8,1,128,256]{3,2,1,0:T(8,128)S(1)}, f32[8,1,128,256]{3,2,1,0:T(8,128)}, u32[]{:S(2)}) copy-start(f32[8,1,128,256]{3,2,1,0:T(8,128)} %param.6) | copy-start | bytes 3145732
  17.8 190.6 %all-reduce.24.cloned.1.call-start = ((), (), s32[]{:S(2)}) async-start(), calls=%async_computation.1 | async-start | bytes 262144 | tf_op jit(solution)/shard_map/psum | solution.py:11
  135.8 187.3 %all-reduce.26.cloned.1.call-start = ((), (), s32[]{:S(2)}) async-start(), calls=%async_computation.2 | async-start | bytes 1048576 | tf_op jit(solution)/shard_map/psum | solution.py:36
  211.3 186.1 %all-reduce.28.cloned.1.call-start = ((), (), s32[]{:S(2)}) async-start(), calls=%async_computation.3 | async-start | bytes 262144 | tf_op jit(solution)/shard_map/psum | solution.py:11
  325.0 187.1 %all-reduce.30.cloned.1.call-start = ((), (), s32[]{:S(2)}) async-start(), calls=%async_computation.4 | async-start | bytes 1048576 | tf_op jit(solution)/shard_map/psum | solution.py:36
  400.4 185.9 %all-reduce.32.cloned.1.call-start = ((), (), s32[]{:S(2)}) async-start(), calls=%async_computation.5 | async-start | bytes 262144 | tf_op jit(solution)/shard_map/psum | solution.py:11
  514.0 187.1 %all-reduce.34.cloned.1.call-start = ((), (), s32[]{:S(2)}) async-start(), calls=%async_computation.6 | async-start | bytes 1048576 | tf_op jit(solution)/shard_map/psum | solution.py:36
  589.4 186.1 %all-reduce.36.cloned.1.call-start = ((), (), s32[]{:S(2)}) async-start(), calls=%async_computation.7 | async-start | bytes 262144 | tf_op jit(solution)/shard_map/psum | solution.py:11
  703.0 187.4 %all-reduce.38.cloned.1.call-start = ((), (), s32[]{:S(2)}) async-start(), calls=%async_computation.8 | async-start | bytes 1048576 | tf_op jit(solution)/shard_map/psum | solution.py:36
  778.7 185.9 %all-reduce.40.cloned.1.call-start = ((), (), s32[]{:S(2)}) async-start(), calls=%async_computation.9 | async-start | bytes 262144 | tf_op jit(solution)/shard_map/psum | solution.py:11
  892.3 187.3 %all-reduce.42.cloned.1.call-start = ((), (), s32[]{:S(2)}) async-start(), calls=%async_computation.10 | async-start | bytes 1048576 | tf_op jit(solution)/shard_map/psum | solution.py:36
  967.9 186.0 %all-reduce.44.cloned.1.call-start = ((), (), s32[]{:S(2)}) async-start(), calls=%async_computation.11 | async-start | bytes 262144 | tf_op jit(solution)/shard_map/psum | solution.py:11
  1081.5 187.4 %all-reduce.46.cloned.1.call-start = ((), (), s32[]{:S(2)}) async-start(), calls=%async_computation.12 | async-start | bytes 1048576 | tf_op jit(solution)/shard_map/psum | solution.py:36
  1157.2 186.0 %all-reduce.48.cloned.1.call-start = ((), (), s32[]{:S(2)}) async-start(), calls=%async_computation.13 | async-start | bytes 262144 | tf_op jit(solution)/shard_map/psum | solution.py:11
  1270.8 122.7 %all-gather.15.cloned.1.call-start = ((), (), s32[]{:S(2)}) async-start(), calls=%async_computation.21 | async-start | bytes 2162688 | tf_op jit(solution)/shard_map/all_gather | solution.py:72
  1345.1 125.1 %all-reduce.50.cloned.1.call-start = ((), (), s32[]{:S(2)}) async-start(), calls=%async_computation.14 | async-start | bytes 262144 | tf_op jit(solution)/shard_map/psum | solution.py:67
  1398.4 122.4 %all-gather.17.cloned.1.call-start = ((), (), s32[]{:S(2)}) async-start(), calls=%async_computation.22 | async-start | bytes 2162688 | tf_op jit(solution)/shard_map/all_gather | solution.py:72
  1472.1 125.5 %all-reduce.52.cloned.1.call-start = ((), (), s32[]{:S(2)}) async-start(), calls=%async_computation.15 | async-start | bytes 262144 | tf_op jit(solution)/shard_map/psum | solution.py:67
  1525.8 122.3 %all-gather.19.cloned.1.call-start = ((), (), s32[]{:S(2)}) async-start(), calls=%async_computation.23 | async-start | bytes 2162688 | tf_op jit(solution)/shard_map/all_gather | solution.py:72
  1599.6 125.4 %all-reduce.54.cloned.1.call-start = ((), (), s32[]{:S(2)}) async-start(), calls=%async_computation.16 | async-start | bytes 262144 | tf_op jit(solution)/shard_map/psum | solution.py:67
  1653.2 122.6 %all-gather.21.cloned.1.call-start = ((), (), s32[]{:S(2)}) async-start(), calls=%async_computation.24 | async-start | bytes 2162688 | tf_op jit(solution)/shard_map/all_gather | solution.py:72
  1727.0 125.9 %all-reduce.56.cloned.1.call-start = ((), (), s32[]{:S(2)}) async-start(), calls=%async_computation.17 | async-start | bytes 262144 | tf_op jit(solution)/shard_map/psum | solution.py:67
  1781.0 122.3 %all-gather.23.cloned.1.call-start = ((), (), s32[]{:S(2)}) async-start(), calls=%async_computation.25 | async-start | bytes 2162688 | tf_op jit(solution)/shard_map/all_gather | solution.py:72
  1854.8 125.7 %all-reduce.58.cloned.1.call-start = ((), (), s32[]{:S(2)}) async-start(), calls=%async_computation.18 | async-start | bytes 262144 | tf_op jit(solution)/shard_map/psum | solution.py:67
  1908.7 122.6 %all-gather.25.cloned.1.call-start = ((), (), s32[]{:S(2)}) async-start(), calls=%async_computation.26 | async-start | bytes 2162688 | tf_op jit(solution)/shard_map/all_gather | solution.py:72
  1982.5 126.1 %all-reduce.60.cloned.1.call-start = ((), (), s32[]{:S(2)}) async-start(), calls=%async_computation.19 | async-start | bytes 262144 | tf_op jit(solution)/shard_map/psum | solution.py:67
  2036.8 122.1 %all-gather.27.cloned.1.call-start = ((), (), s32[]{:S(2)}) async-start(), calls=%async_computation.27 | async-start | bytes 2162688 | tf_op jit(solution)/shard_map/all_gather | solution.py:72
  2110.6 125.8 %all-reduce.62.cloned.1.call-start = ((), (), s32[]{:S(2)}) async-start(), calls=%async_computation.20 | async-start | bytes 262144 | tf_op jit(solution)/shard_map/psum | solution.py:67
  2162.2 75.6 %copy-start.8 = (f32[256,128]{1,0:T(8,128)S(1)}, f32[256,128]{1,0:T(8,128)}, u32[]{:S(2)}) copy-start(f32[256,128]{1,0:T(8,128)} %get-tuple-element.37) | copy-start | bytes 393220
  2162.2 75.6 %copy-start.7 = (f32[256,128]{1,0:T(8,128)S(1)}, f32[256,128]{1,0:T(8,128)}, u32[]{:S(2)}) copy-start(f32[256,128]{1,0:T(8,128)} %get-tuple-element.35) | copy-start | bytes 393220
  (7 other events, 521.5 us)
Sparse Core Ops, SparseCore 0:
  17.9 116.0 all-reduce.21
  136.4 71.9 all-reduce.23
  211.6 111.5 all-reduce.25
  325.4 71.9 all-reduce.27
  400.5 111.5 all-reduce.29
  514.4 71.9 all-reduce.31
  589.5 111.5 all-reduce.33
  703.5 71.9 all-reduce.35
  778.8 111.5 all-reduce.37
  892.7 71.9 all-reduce.39
  968.0 111.5 all-reduce.41
  1081.9 71.9 all-reduce.43
  1157.3 111.5 all-reduce.45
  1271.2 71.9 all-reduce.47
  1345.5 47.9 all-gather.14
  1398.5 71.6 all-reduce.49
  1472.8 47.9 all-gather.16
  1525.9 71.6 all-reduce.51
  1600.1 47.9 all-gather.18
  1653.3 71.6 all-reduce.53
  1727.8 47.9 all-gather.20
  1781.1 71.6 all-reduce.55
  1855.3 47.9 all-gather.22
  1908.8 71.6 all-reduce.57
  1983.3 47.9 all-gather.24
  2036.9 71.6 all-reduce.59
  2110.9 47.9 all-gather.26
  2164.7 71.6 all-reduce.61
where the time goes:
time: 2250 us
  waiting for transfers between devices  2130 us (95%)
  matrix products  58.4 us (3%)
  local copies, waits for them, and re-layouts  23.5 us (1%)
    psum x7, waiting for transfers between devices, per_device(): row_total = lax.psum(partial_sum, 'col')  786 us
    psum x7, waiting for transfers between devices, spread(): return lax.psum(kept, axis)  507 us
    psum x7, waiting for transfers between devices, per_device(): resid = resid - lax.psum(partial_sum, 'row')  502 us
    all_gather x7, waiting for transfers between devices, per_device(): pieces = lax.all_gather(low_solved[None], 'col', axis=0, tiled=True)  339 us
  transfers between devices with their start and end apart: 28, of which 28 were waited for; matrix products, arithmetic and copies ran while one was open for 0% of the time, Pallas kernels for 0%

commit v1 on v0

--- a/solution.py
+++ b/solution.py
@@ -33,7 +33,16 @@
             partial_sum = jnp.einsum(
                 "abpq,bqs->aps", panel, earlier, preferred_element_type=jnp.float32
             )
-            row_total = lax.psum(partial_sum, "col")
+
+            def convert_loops(local_block):
+                wide_n = jax.lax.axis_size("col")
+                base_arr = lambda piece_next: [(k, k ^ piece_next) for k in range(wide_n)]
+                state_now = local_block
+                for src_i in range(wide_n.bit_length() - 1):
+                    state_now = state_now + jax.lax.ppermute(state_now, "col", base_arr(1 << src_i))
+                return state_now
+
+            row_total = convert_loops(partial_sum)
             row_total = row_total.reshape((per_col, groups) + row_total.shape[1:])
             own_total = lax.dynamic_index_in_dim(
                 row_total, my_col // row_count, axis=1, keepdims=False

time: 2250 us -> 1840 us (0.82)
  waiting for transfers between devices: 2130 us -> 1680 us
  starting transfers between devices: 1.32 us -> 54.2 us
    psum x7 -> x0, waiting for transfers between devices: 786 us -> none  [per_device(): row_total = lax.psum(partial_sum, 'col')]
    ppermute x0 -> x35, waiting for transfers between devices: none -> 343 us  [convert_loops(): jax.lax.ppermute(state_now, 'col', base_arr(1 << src_i))]
    ppermute x0 -> x35, starting transfers between devices: none -> 53.1 us  [convert_loops(): jax.lax.ppermute(state_now, 'col', base_arr(1 << src_i))]
  transfers between devices with their start and end apart: 28 -> 56, of which waited for: 28 -> 56; matrix products, arithmetic and copies ran while one was open for 0% -> 0% of each run, Pallas kernels for 0% -> 0%
where the time goes in v1:
time: 1840 us; the launch traced here: 1830 us
  waiting for transfers between devices  1680 us (91%)
  starting transfers between devices  54.2 us (3%)
  matrix products  46.7 us (3%)
  local copies, waits for them, and re-layouts  23.5 us (1%)
    psum x7, waiting for transfers between devices, per_device(): resid = resid - lax.psum(partial_sum, 'row')  502 us
    psum x7, waiting for transfers between devices, spread(): return lax.psum(kept, axis)  493 us
    ppermute x35, waiting for transfers between devices, convert_loops(): jax.lax.ppermute(state_now, 'col', base_arr(1 << src_i))  343 us
    all_gather x7, waiting for transfers between devices, per_device(): pieces = lax.all_gather(low_solved[None], 'col', axis=0, tiled=True)  339 us
    ppermute x35, starting transfers between devices, convert_loops(): jax.lax.ppermute(state_now, 'col', base_arr(1 << src_i))  53.1 us
  transfers between devices with their start and end apart: 56, of which 56 were waited for; matrix products, arithmetic and copies ran while one was open for 0% of the time, Pallas kernels for 0%

profile of v1, /device:TPU:2, one launch (start us, length us, event | category | flops | bytes accessed | tf_op | source)
XLA Modules:
  0.0 1832.8 jit_solution(3501886412860637948)
XLA Ops:
  35.3 13.4 collective-permute-done.2
  75.7 73.4 %all-reduce.15.cloned.1.call-done = f32[1,128,256]{2,1,0:T(8,128)} async-done(((f32[1,128,256]{2,1,0:T(8,128)}), f32[1,128,256]{2,1,0:T(8,128)}) %all-reduce.15.cloned.1.call-update) | async-done | bytes 131088 | tf_op jit(solution)/shard_map/psum | solution.py:11
  153.9 13.4 collective-permute-done.6
  208.9 69.9 %all-reduce.17.cloned.1.call-done = f32[1,128,256]{2,1,0:T(8,128)} async-done(((f32[1,128,256]{2,1,0:T(8,128)}), f32[1,128,256]{2,1,0:T(8,128)}) %all-reduce.17.cloned.1.call-update) | async-done | bytes 131088 | tf_op jit(solution)/shard_map/psum | solution.py:11
  283.8 13.4 collective-permute-done.11
  299.4 12.6 collective-permute-done.12
  338.8 70.0 %all-reduce.19.cloned.1.call-done = f32[1,128,256]{2,1,0:T(8,128)} async-done(((f32[1,128,256]{2,1,0:T(8,128)}), f32[1,128,256]{2,1,0:T(8,128)}) %all-reduce.19.cloned.1.call-update) | async-done | bytes 131088 | tf_op jit(solution)/shard_map/psum | solution.py:11
  414.3 13.4 collective-permute-done.16
  469.3 69.9 %all-reduce.21.cloned.1.call-done = f32[1,128,256]{2,1,0:T(8,128)} async-done(((f32[1,128,256]{2,1,0:T(8,128)}), f32[1,128,256]{2,1,0:T(8,128)}) %all-reduce.21.cloned.1.call-update) | async-done | bytes 131088 | tf_op jit(solution)/shard_map/psum | solution.py:11
  544.3 13.4 collective-permute-done.21
  559.9 12.6 collective-permute-done.22
  599.3 69.9 %all-reduce.23.cloned.1.call-done = f32[1,128,256]{2,1,0:T(8,128)} async-done(((f32[1,128,256]{2,1,0:T(8,128)}), f32[1,128,256]{2,1,0:T(8,128)}) %all-reduce.23.cloned.1.call-update) | async-done | bytes 131088 | tf_op jit(solution)/shard_map/psum | solution.py:11
  674.4 13.4 collective-permute-done.26
  690.1 12.6 collective-permute-done.27
  729.4 70.0 %all-reduce.25.cloned.1.call-done = f32[1,128,256]{2,1,0:T(8,128)} async-done(((f32[1,128,256]{2,1,0:T(8,128)}), f32[1,128,256]{2,1,0:T(8,128)}) %all-reduce.25.cloned.1.call-update) | async-done | bytes 131088 | tf_op jit(solution)/shard_map/psum | solution.py:11
  804.7 13.4 collective-permute-done.31
  820.5 12.6 collective-permute-done.32
  859.9 69.9 %all-reduce.27.cloned.1.call-done = f32[128,256]{1,0:T(8,128)} async-done(((f32[128,256]{1,0:T(8,128)}), f32[128,256]{1,0:T(8,128)}) %all-reduce.27.cloned.1.call-update) | async-done | bytes 131088 | tf_op jit(solution)/shard_map/psum | solution.py:11
  931.8 48.7 %all-gather.15.cloned.1.call-done = bf16[4096,256]{0,1:T(8,128)(2,1)} async-done(((bf16[128,256]{0,1:T(8,128)(2,1)}), bf16[4096,256]{0,1:T(8,128)(2,1)}) %all-gather.15.cloned.1.call-update) | async-done | bytes 2097168 | tf_op jit(solution)/shard_map/all_gather | solution.py:81
  985.5 71.8 %all-reduce.29.cloned.1.call-done = f32[1,128,256]{2,1,0:T(8,128)} async-done(((f32[1,128,256]{2,1,0:T(8,128)}), f32[1,128,256]{2,1,0:T(8,128)}) %all-reduce.29.cloned.1.call-update) | async-done | bytes 131088 | tf_op jit(solution)/shard_map/psum | solution.py:76
  1059.3 48.3 %all-gather.17.cloned.1.call-done = bf16[4096,256]{0,1:T(8,128)(2,1)} async-done(((bf16[128,256]{0,1:T(8,128)(2,1)}), bf16[4096,256]{0,1:T(8,128)(2,1)}) %all-gather.17.cloned.1.call-update) | async-done | bytes 2097168 | tf_op jit(solution)/shard_map/all_gather | solution.py:81
  1112.6 71.8 %all-reduce.31.cloned.1.call-done = f32[1,128,256]{2,1,0:T(8,128)} async-done(((f32[1,128,256]{2,1,0:T(8,128)}), f32[1,128,256]{2,1,0:T(8,128)}) %all-reduce.31.cloned.1.call-update) | async-done | bytes 131088 | tf_op jit(solution)/shard_map/psum | solution.py:76
  1186.4 48.6 %all-gather.19.cloned.1.call-done = bf16[4096,256]{0,1:T(8,128)(2,1)} async-done(((bf16[128,256]{0,1:T(8,128)(2,1)}), bf16[4096,256]{0,1:T(8,128)(2,1)}) %all-gather.19.cloned.1.call-update) | async-done | bytes 2097168 | tf_op jit(solution)/shard_map/all_gather | solution.py:81
  1240.2 71.8 %all-reduce.33.cloned.1.call-done = f32[1,128,256]{2,1,0:T(8,128)} async-done(((f32[1,128,256]{2,1,0:T(8,128)}), f32[1,128,256]{2,1,0:T(8,128)}) %all-reduce.33.cloned.1.call-update) | async-done | bytes 131088 | tf_op jit(solution)/shard_map/psum | solution.py:76
  1313.9 48.3 %all-gather.21.cloned.1.call-done = bf16[4096,256]{0,1:T(8,128)(2,1)} async-done(((bf16[128,256]{0,1:T(8,128)(2,1)}), bf16[4096,256]{0,1:T(8,128)(2,1)}) %all-gather.21.cloned.1.call-update) | async-done | bytes 2097168 | tf_op jit(solution)/shard_map/all_gather | solution.py:81
  1367.6 71.8 %all-reduce.35.cloned.1.call-done = f32[1,128,256]{2,1,0:T(8,128)} async-done(((f32[1,128,256]{2,1,0:T(8,128)}), f32[1,128,256]{2,1,0:T(8,128)}) %all-reduce.35.cloned.1.call-update) | async-done | bytes 131088 | tf_op jit(solution)/shard_map/psum | solution.py:76
  1441.4 48.6 %all-gather.23.cloned.1.call-done = bf16[4096,256]{0,1:T(8,128)(2,1)} async-done(((bf16[128,256]{0,1:T(8,128)(2,1)}), bf16[4096,256]{0,1:T(8,128)(2,1)}) %all-gather.23.cloned.1.call-update) | async-done | bytes 2097168 | tf_op jit(solution)/shard_map/all_gather | solution.py:81
  1495.4 71.8 %all-reduce.37.cloned.1.call-done = f32[1,128,256]{2,1,0:T(8,128)} async-done(((f32[1,128,256]{2,1,0:T(8,128)}), f32[1,128,256]{2,1,0:T(8,128)}) %all-reduce.37.cloned.1.call-update) | async-done | bytes 131088 | tf_op jit(solution)/shard_map/psum | solution.py:76
  1569.4 48.0 %all-gather.25.cloned.1.call-done = bf16[4096,256]{0,1:T(8,128)(2,1)} async-done(((bf16[128,256]{0,1:T(8,128)(2,1)}), bf16[4096,256]{0,1:T(8,128)(2,1)}) %all-gather.25.cloned.1.call-update) | async-done | bytes 2097168 | tf_op jit(solution)/shard_map/all_gather | solution.py:81
  1623.1 71.8 %all-reduce.39.cloned.1.call-done = f32[1,128,256]{2,1,0:T(8,128)} async-done(((f32[1,128,256]{2,1,0:T(8,128)}), f32[1,128,256]{2,1,0:T(8,128)}) %all-reduce.39.cloned.1.call-update) | async-done | bytes 131088 | tf_op jit(solution)/shard_map/psum | solution.py:76
  1696.9 48.5 %all-gather.27.cloned.1.call-done = bf16[4096,256]{0,1:T(8,128)(2,1)} async-done(((bf16[128,256]{0,1:T(8,128)(2,1)}), bf16[4096,256]{0,1:T(8,128)(2,1)}) %all-gather.27.cloned.1.call-update) | async-done | bytes 2097168 | tf_op jit(solution)/shard_map/all_gather | solution.py:81
  1751.1 71.8 %all-reduce.41.cloned.1.call-done = f32[1,128,256]{2,1,0:T(8,128)} async-done(((f32[1,128,256]{2,1,0:T(8,128)}), f32[1,128,256]{2,1,0:T(8,128)}) %all-reduce.41.cloned.1.call-update) | async-done | bytes 131088 | tf_op jit(solution)/shard_map/psum | solution.py:76
  (242 shorter events, 339.4 us)
Async XLA Ops:
  6.5 142.6 %all-reduce.15.cloned.1.call-start = ((), (), s32[]{:S(2)}) async-start(), calls=%async_computation | async-start | bytes 262144 | tf_op jit(solution)/shard_map/psum | solution.py:11
  19.0 14.6 collective-permute-start.1
  33.6 15.0 collective-permute-start.2
  75.7 203.2 %all-reduce.17.cloned.1.call-start = ((), (), s32[]{:S(2)}) async-start(), calls=%async_computation.1 | async-start | bytes 262144 | tf_op jit(solution)/shard_map/psum | solution.py:11
  167.4 14.7 collective-permute-start.7
  208.9 199.9 %all-reduce.19.cloned.1.call-start = ((), (), s32[]{:S(2)}) async-start(), calls=%async_computation.2 | async-start | bytes 262144 | tf_op jit(solution)/shard_map/psum | solution.py:11
  283.2 14.1 collective-permute-start.11
  297.3 14.7 collective-permute-start.12
  338.8 200.4 %all-reduce.21.cloned.1.call-start = ((), (), s32[]{:S(2)}) async-start(), calls=%async_computation.3 | async-start | bytes 262144 | tf_op jit(solution)/shard_map/psum | solution.py:11
  413.6 14.1 collective-permute-start.16
  427.7 14.7 collective-permute-start.17
  469.2 200.0 %all-reduce.23.cloned.1.call-start = ((), (), s32[]{:S(2)}) async-start(), calls=%async_computation.4 | async-start | bytes 262144 | tf_op jit(solution)/shard_map/psum | solution.py:11
  543.7 14.1 collective-permute-start.21
  557.8 14.7 collective-permute-start.22
  599.3 200.2 %all-reduce.25.cloned.1.call-start = ((), (), s32[]{:S(2)}) async-start(), calls=%async_computation.5 | async-start | bytes 262144 | tf_op jit(solution)/shard_map/psum | solution.py:11
  687.9 14.7 collective-permute-start.27
  729.4 200.4 %all-reduce.27.cloned.1.call-start = ((), (), s32[]{:S(2)}) async-start(), calls=%async_computation.6 | async-start | bytes 262144 | tf_op jit(solution)/shard_map/psum | solution.py:11
  818.2 14.9 collective-permute-start.32
  859.8 120.7 %all-gather.15.cloned.1.call-start = ((), (), s32[]{:S(2)}) async-start(), calls=%async_computation.14 | async-start | bytes 2162688 | tf_op jit(solution)/shard_map/all_gather | solution.py:81
  931.7 125.6 %all-reduce.29.cloned.1.call-start = ((), (), s32[]{:S(2)}) async-start(), calls=%async_computation.7 | async-start | bytes 262144 | tf_op jit(solution)/shard_map/psum | solution.py:76
  985.5 122.1 %all-gather.17.cloned.1.call-start = ((), (), s32[]{:S(2)}) async-start(), calls=%async_computation.15 | async-start | bytes 2162688 | tf_op jit(solution)/shard_map/all_gather | solution.py:81
  1059.2 125.2 %all-reduce.31.cloned.1.call-start = ((), (), s32[]{:S(2)}) async-start(), calls=%async_computation.8 | async-start | bytes 262144 | tf_op jit(solution)/shard_map/psum | solution.py:76
  1112.6 122.4 %all-gather.19.cloned.1.call-start = ((), (), s32[]{:S(2)}) async-start(), calls=%async_computation.16 | async-start | bytes 2162688 | tf_op jit(solution)/shard_map/all_gather | solution.py:81
  1186.4 125.6 %all-reduce.33.cloned.1.call-start = ((), (), s32[]{:S(2)}) async-start(), calls=%async_computation.9 | async-start | bytes 262144 | tf_op jit(solution)/shard_map/psum | solution.py:76
  1240.1 122.1 %all-gather.21.cloned.1.call-start = ((), (), s32[]{:S(2)}) async-start(), calls=%async_computation.17 | async-start | bytes 2162688 | tf_op jit(solution)/shard_map/all_gather | solution.py:81
  1313.9 125.4 %all-reduce.35.cloned.1.call-start = ((), (), s32[]{:S(2)}) async-start(), calls=%async_computation.10 | async-start | bytes 262144 | tf_op jit(solution)/shard_map/psum | solution.py:76
  1367.5 122.4 %all-gather.23.cloned.1.call-start = ((), (), s32[]{:S(2)}) async-start(), calls=%async_computation.18 | async-start | bytes 2162688 | tf_op jit(solution)/shard_map/all_gather | solution.py:81
  1441.3 125.9 %all-reduce.37.cloned.1.call-start = ((), (), s32[]{:S(2)}) async-start(), calls=%async_computation.11 | async-start | bytes 262144 | tf_op jit(solution)/shard_map/psum | solution.py:76
  1495.3 122.1 %all-gather.25.cloned.1.call-start = ((), (), s32[]{:S(2)}) async-start(), calls=%async_computation.19 | async-start | bytes 2162688 | tf_op jit(solution)/shard_map/all_gather | solution.py:81
  1569.2 125.7 %all-reduce.39.cloned.1.call-start = ((), (), s32[]{:S(2)}) async-start(), calls=%async_computation.12 | async-start | bytes 262144 | tf_op jit(solution)/shard_map/psum | solution.py:76
  1623.0 122.4 %all-gather.27.cloned.1.call-start = ((), (), s32[]{:S(2)}) async-start(), calls=%async_computation.20 | async-start | bytes 2162688 | tf_op jit(solution)/shard_map/all_gather | solution.py:81
  1696.8 126.1 %all-reduce.41.cloned.1.call-start = ((), (), s32[]{:S(2)}) async-start(), calls=%async_computation.13 | async-start | bytes 262144 | tf_op jit(solution)/shard_map/psum | solution.py:76
  (35 other events, 991.1 us)
Sparse Core Ops, SparseCore 0:
  75.8 73.2 all-reduce.14
  209.0 69.8 all-reduce.16
  338.9 69.8 all-reduce.18
  469.3 69.8 all-reduce.20
  599.4 69.8 all-reduce.22
  729.5 69.8 all-reduce.24
  859.9 69.8 all-reduce.26
  932.6 47.9 all-gather.14
  985.6 71.6 all-reduce.28
  1059.6 47.9 all-gather.16
  1112.7 71.6 all-reduce.30
  1187.0 47.9 all-gather.18
  1240.2 71.6 all-reduce.32
  1314.3 47.9 all-gather.20
  1367.6 71.6 all-reduce.34
  1442.0 47.9 all-gather.22
  1495.5 71.6 all-reduce.36
  1569.5 47.9 all-gather.24
  1623.1 71.6 all-reduce.38
  1697.4 47.9 all-gather.26
  1751.3 71.6 all-reduce.40
